TPU v7x, 32 devices: a whole 2x2x4 slice. The times are simulated.
32 devices in a mesh: pipe: 4 (over y, x), dp: 8 (over z, core).
Axes of the slice: x: 2, y: 2, z: 4, core: 2. Of those that a mesh axis runs over, the one named last changes fastest.
Arguments:
- cotangent: bfloat16 [4, 1024, 6144], P('pipe', 'dp'), may hold values from -0.29882812 to 0.29882812
- slot_token: int32 [4, 8, 24], P('pipe', 'dp'), may hold values from 0 to 127, as said below
- slot_count: int32 [4, 8], P('pipe', 'dp'), may hold values from 6 to 24, as said below
- slot_weight: float32 [4, 8, 24], P('pipe', 'dp'), may hold values from 0.1 to 0.9
- hidden: bfloat16 [4, 8, 24, 8192], P('pipe', 'dp'), may hold values from -6 to 6
Outputs:
- down_grad: bfloat16 [4, 8192, 6144], P('pipe', 'dp')
Inputs may be any that keep to these rules, and one draw needn't show every extreme that they name: `slot_token`: within one device's 24 slots of a section the token indices are distinct. `slot_count`: in every section some device has all 24 slots live.
All inputs are finite; a program needn't handle non-finite values.
Results may differ from a plain program's by a relative error of at most 0.0049.
Values may be sent and summed in bfloat16 or wider, within the bound.
No kernel may reach another device: no remote copies, remote signals or barrier semaphores. Data moves between devices by JAX's collectives and lax.ppermute only.
A program may use at most 128 MiB of HBM per device.

v0:
```python
import jax
import jax.numpy as jnp
from jax import lax
from jax.sharding import PartitionSpec as P


def shifted(value, axis, steps):
    count = lax.axis_size(axis)
    pairs = [(source, (source + steps) % count) for source in range(count)]
    return lax.ppermute(value, axis, pairs)


def select_rows(table, positions):
    return jnp.take(table[0], positions.reshape(-1), axis=0)


def local(cotangent, slot_token, slot_count, slot_weight, hidden):
    slots = slot_token.shape[2]
    slot_pos = lax.broadcasted_iota(jnp.int32, (slots,), 0)
    live_mask = (slot_pos < slot_count[0, 0]).astype(jnp.float32)
    ahead_tokens = shifted(slot_token, "pipe", 1)
    prepared = select_rows(cotangent, ahead_tokens)
    picked = shifted(prepared, "pipe", -1)
    factors = slot_weight[0, 0] * live_mask
    scaled_rows = (factors[:, None] * picked.astype(jnp.float32)).astype(jnp.bfloat16)[None]
    exchanged = lax.all_to_all(hidden, "dp", split_axis=3, concat_axis=1, tiled=True)[0]
    gathered = lax.all_gather(scaled_rows, "dp", axis=0, tiled=True)
    width = gathered.shape[2]
    flat_rows = gathered.reshape(-1, width)
    flat_hidden = exchanged.reshape(-1, exchanged.shape[2])
    summed = lax.dot_general(
        flat_hidden, flat_rows, (((0,), (0,)), ((), ())), preferred_element_type=jnp.float32
    )
    return summed.astype(jnp.bfloat16)[None]


def solution(mesh):
    placed = (
        P("pipe", "dp", None),
        P("pipe", "dp", None),
        P("pipe", "dp"),
        P("pipe", "dp", None),
        P("pipe", "dp", None, None),
    )
    return jax.shard_map(
        local, mesh=mesh, in_specs=placed, out_specs=P("pipe", "dp", None), check_vma=False
    )
```

profile of v0, /device:TPU:0, one launch (start us, length us, event | category | flops | bytes accessed | tf_op | source)
XLA Modules:
  0.0 143.8 jit_solution(2741923419532207530)
XLA Ops:
  6.5 0.0 copy-start
  6.5 0.0 copy-start.2
  6.5 0.0 copy-start.1
  6.5 0.0 all-gather.3.cloned.1.call-start
  6.5 3.0 %collective-permute-start = (s32[1,1,24]{2,1,0:T(1,128)}, s32[1,1,24]{2,1,0:T(1,128)S(1)}, u32[]{:S(2)}, u32[]{:S(2)}) collective-permute-start(s32[1,1,24]{2,1,0:T(1,128)} %param.6), channel_id=1, source_target_pairs={{0,8},{8,16},{16,24},{24,0},{1,9},{9,17},{17,25},{25,1},{2,10},{10... | collective-permute-start | bytes 296 | tf_op jit(solution)/shard_map/ppermute | solution.py:10
  9.6 2.6 %collective-permute-done = s32[1,1,24]{2,1,0:T(1,128)S(1)} collective-permute-done((s32[1,1,24]{2,1,0:T(1,128)}, s32[1,1,24]{2,1,0:T(1,128)S(1)}, u32[]{:S(2)}, u32[]{:S(2)}) %collective-permute-start) | collective-permute-done | bytes 128 | tf_op jit(solution)/shard_map/ppermute | solution.py:10
  12.2 0.0 copy-done
  12.2 0.7 gather_fusion
  13.0 0.1 broadcast_select_fusion
  13.1 2.1 %collective-permute-start.1 = (bf16[24,6144]{1,0:T(8,128)(2,1)S(1)}, bf16[24,6144]{1,0:T(8,128)(2,1)S(1)}, u32[]{:S(2)}, u32[]{:S(2)}) collective-permute-start(bf16[24,6144]{1,0:T(8,128)(2,1)S(1)} %broadcast_select_fusion), channel_id=1, source_target_pairs={{0,24},{8,0},{16,8},{24,16},{1,25},{9,1},{17,9},{25,17},{2,26},{10... | collective-permute-start | bytes 884744 | tf_op jit(solution)/shard_map/ppermute | solution.py:10
  15.8 0.0 copy-done.2
  15.8 5.2 %collective-permute-done.1 = bf16[24,6144]{1,0:T(8,128)(2,1)S(1)} collective-permute-done((bf16[24,6144]{1,0:T(8,128)(2,1)S(1)}, bf16[24,6144]{1,0:T(8,128)(2,1)S(1)}, u32[]{:S(2)}, u32[]{:S(2)}) %collective-permute-start.1) | collective-permute-done | bytes 294944 | tf_op jit(solution)/shard_map/ppermute | solution.py:10
  21.0 0.8 multiply_convert_fusion
  21.8 0.0 all-gather.3.cloned.1.call-update
  21.9 0.0 copy-done.1
  21.9 6.7 %copy.10 = bf16[1,1,24,8192]{2,1,0,3:T(2,128)(2,1)} copy(bf16[1,1,24,8192]{3,2,1,0:T(8,128)(2,1)S(1)} %copy-done.1) | data formatting | bytes 786432 | tf_op args[4]
  28.5 0.6 broadcast.49
  29.1 46.6 %reduce = bf16[8192,24]{1,0:T(8,128)(2,1)} reduce(bf16[8192,1,1,24]{3,2,1,0:T(2,128)(2,1)} %bitcast.28, bf16[]{:T(256)} %broadcast.49), dimensions={1,2}, to_apply=%bitcast.22.reduce_sub_computation | reduce | bytes 786434
  75.6 3.9 %reshape.65 = bf16[8,2,12288]{2,1,0:T(2,128)(2,1)S(1)} reshape(bf16[8192,24]{1,0:T(8,128)(2,1)} %reduce) | data formatting | bytes 786432
  79.6 17.4 %all_to_all.15 = bf16[8,2,12288]{2,1,0:T(2,128)(2,1)S(1)} all-to-all(bf16[8,2,12288]{2,1,0:T(2,128)(2,1)S(1)} %reshape.65), channel_id=1, replica_groups=mesh['pipe'=4,'dp'=8] {'dp'}, dimensions={0} | all-to-all | bytes 786432 | tf_op jit(solution)/shard_map/all_to_all | solution.py:26
  96.9 6.6 %reshape.66 = bf16[8192,1,1,24]{3,2,1,0:T(2,128)(2,1)} reshape(bf16[8,2,12288]{2,1,0:T(2,128)(2,1)S(1)} %all_to_all.15) | data formatting | bytes 786432
  103.6 8.0 %copy.11 = bf16[1,1,24,8192]{3,2,1,0:T(8,128)(2,1)S(1)} copy(bf16[1,1,24,8192]{2,1,0,3:T(2,128)(2,1)} %bitcast.29) | data formatting | bytes 786432 | tf_op jit(solution)/shard_map/all_to_all | solution.py:26
  111.6 0.2 copy.14
  111.8 0.2 copy.12
  112.1 0.0 all-gather.3.cloned.1.call-done
  112.1 8.3 %convert_bitcast_fusion = bf16[1,1024,6144]{1,2,0:T(8,128)(2,1)} fusion(bf16[192,6144]{1,0:T(8,128)(2,1)} %all-gather.3.cloned.1.call-done, bf16[192,1024]{1,0:T(8,128)(2,1)S(1)} %bitcast.32), kind=kOutput, calls=%fused_computation.1 | convolution fusion | flops 2422210560 | bytes 15335424 | tf_op jit(solution)/shard_map/dot_general | solution.py:31
  120.4 16.6 %copy.13 = bf16[1,1024,6144]{2,1,0:T(8,128)(2,1)} copy(bf16[1,1024,6144]{1,2,0:T(8,128)(2,1)} %convert_bitcast_fusion) | data formatting | bytes 25165824 | tf_op jit(solution)/shard_map/broadcast_in_dim | solution.py:34
  (4 shorter events, 0.0 us)
Async XLA Ops:
  6.5 5.7 %copy-start = (bf16[1,128,6144]{2,1,0:T(8,128)(2,1)S(1)}, bf16[1,128,6144]{2,1,0:T(8,128)(2,1)}, u32[]{:S(2)}) copy-start(bf16[1,128,6144]{2,1,0:T(8,128)(2,1)} %param.5) | copy-start | bytes 4718596
  6.5 9.3 %copy-start.2 = (f32[1,1,24]{2,1,0:T(1,128)S(1)}, f32[1,1,24]{2,1,0:T(1,128)}, u32[]{:S(2)}) copy-start(f32[1,1,24]{2,1,0:T(1,128)} %param.8) | copy-start | bytes 292
  6.5 15.3 %copy-start.1 = (bf16[1,1,24,8192]{3,2,1,0:T(8,128)(2,1)S(1)}, bf16[1,1,24,8192]{3,2,1,0:T(8,128)(2,1)}, u32[]{:S(2)}) copy-start(bf16[1,1,24,8192]{3,2,1,0:T(8,128)(2,1)} %param.9) | copy-start | bytes 1179652
  6.5 105.5 %all-gather.3.cloned.1.call-start = ((), (), s32[]{:S(2)}) async-start(), calls=%async_computation.1 | async-start | bytes 2654208 | tf_op jit(solution)/shard_map/all_gather | solution.py:27
  6.5 5.7 %collective-permute-start = (s32[1,1,24]{2,1,0:T(1,128)}, s32[1,1,24]{2,1,0:T(1,128)S(1)}, u32[]{:S(2)}, u32[]{:S(2)}) collective-permute-start(s32[1,1,24]{2,1,0:T(1,128)} %param.6), channel_id=1, source_target_pairs={{0,8},{8,16},{16,24},{24,0},{1,9},{9,17},{17,25},{25,1},{2,10},{10... | collective-permute-start | bytes 296 | tf_op jit(solution)/shard_map/ppermute | solution.py:10
  13.1 7.9 %collective-permute-start.1 = (bf16[24,6144]{1,0:T(8,128)(2,1)S(1)}, bf16[24,6144]{1,0:T(8,128)(2,1)S(1)}, u32[]{:S(2)}, u32[]{:S(2)}) collective-permute-start(bf16[24,6144]{1,0:T(8,128)(2,1)S(1)} %broadcast_select_fusion), channel_id=1, source_target_pairs={{0,24},{8,0},{16,8},{24,16},{1,25},{9,1},{17,9},{25,17},{2,26},{10... | collective-permute-start | bytes 884744 | tf_op jit(solution)/shard_map/ppermute | solution.py:10
Sparse Core Ops, SparseCore 0:
  22.0 32.8 all-gather.2
where the time goes:
time: 145 us; the launch traced here: 144 us
  other arithmetic  47.5 us (33%)
  local copies, waits for them, and re-layouts  43.5 us (30%)
  blocking collectives  17.4 us (12%)
  between operations  14.1 us (10%)
  matrix products  8.29 us (6%)
  waiting for transfers between devices  7.86 us (5%)
  starting transfers between devices  5.09 us (4%)
    unnamed x1, other arithmetic  46.6 us
    unnamed x11, local copies, waits for them, and re-layouts  18 us
    all_to_all x1, blocking collectives, local(): lax.all_to_all(hidden, 'dp', split_axis=3, concat_axis=1, tiled=True)[0]  17.4 us
    broadcast_in_dim x1, local copies, waits for them, and re-layouts, local(): return summed.astype(jnp.bfloat16)[None]  16.6 us
    dot_general x1, matrix products, local(): lax.dot_general(flat_hidden, flat_rows, (((0,), (0,)), ((), ())), preferr...  8.29 us
    all_to_all x2, local copies, waits for them, and re-layouts, local(): lax.all_to_all(hidden, 'dp', split_axis=3, concat_axis=1, tiled=True)[0]  8.22 us
    ppermute x2, waiting for transfers between devices, shifted(): return lax.ppermute(value, axis, pairs)  7.82 us
    ppermute x2, starting transfers between devices, shifted(): return lax.ppermute(value, axis, pairs)  5.09 us
  transfers between devices with their start and end apart: 3, of which 2 were waited for; matrix products, arithmetic and copies ran while one was open for 51% of the time, Pallas kernels for 0%

commit v1 on v0

--- a/solution.py
+++ b/solution.py
@@ -23,7 +23,10 @@
     picked = shifted(prepared, "pipe", -1)
     factors = slot_weight[0, 0] * live_mask
     scaled_rows = (factors[:, None] * picked.astype(jnp.float32)).astype(jnp.bfloat16)[None]
-    exchanged = lax.all_to_all(hidden, "dp", split_axis=3, concat_axis=1, tiled=True)[0]
+    exchanged = jnp.concatenate(
+        lax.all_to_all(jnp.stack(jnp.split(hidden, lax.axis_size("dp"), axis=3)), "dp", 0, 0),
+        axis=1,
+    )[0]
     gathered = lax.all_gather(scaled_rows, "dp", axis=0, tiled=True)
     width = gathered.shape[2]
     flat_rows = gathered.reshape(-1, width)

time: 145 us -> 75.1 us (0.52)
  other arithmetic: 47.5 us -> 0.95 us
  local copies, waits for them, and re-layouts: 43.5 us -> 0.78 us
  waiting for transfers between devices: 7.86 us -> 21.8 us
  blocking collectives: 17.4 us -> 23.9 us
    unnamed x1 -> x0, other arithmetic: 46.6 us -> none
    unnamed x11 -> x13, local copies, waits for them, and re-layouts: 18 us -> 0.05 us
    broadcast_in_dim x1 -> x0, local copies, waits for them, and re-layouts: 16.6 us -> none  [local(): return summed.astype(jnp.bfloat16)[None]]
    all_gather x1, waiting for transfers between devices: 0.02 us -> 14 us  [local(): gathered = lax.all_gather(scaled_rows, 'dp', axis=0, tiled=True)]
    all_to_all x2 -> x0, local copies, waits for them, and re-layouts: 8.22 us -> none  [local(): lax.all_to_all(hidden, 'dp', split_axis=3, concat_axis=1, tiled=True)[0]]
    all_to_all x1, blocking collectives: 17.4 us -> 23.9 us  [local(): lax.all_to_all(jnp.stack(jnp.split(hidden, lax.axis_size('dp'), axis=3)),...]
  transfers between devices with their start and end apart: 3 -> 3, of which waited for: 2 -> 3; matrix products, arithmetic and copies ran while one was open for 51% -> 0% of each run, Pallas kernels for 0% -> 0%
where the time goes in v1:
time: 75.1 us; the launch traced here: 75 us
  blocking collectives  23.9 us (32%)
  waiting for transfers between devices  21.8 us (29%)
  between operations  14.2 us (19%)
  matrix products  8.28 us (11%)
  starting transfers between devices  5.09 us (7%)
  other arithmetic  0.95 us (1%)
  local copies, waits for them, and re-layouts  0.78 us (1%)
    all_to_all x1, blocking collectives, local(): lax.all_to_all(jnp.stack(jnp.split(hidden, lax.axis_size('dp'), axis=3)),...  23.9 us
    all_gather x1, waiting for transfers between devices, local(): gathered = lax.all_gather(scaled_rows, 'dp', axis=0, tiled=True)  14 us
    dot_general x1, matrix products, local(): lax.dot_general(flat_hidden, flat_rows, (((0,), (0,)), ((), ())), preferr...  8.28 us
    ppermute x2, waiting for transfers between devices, shifted(): return lax.ppermute(value, axis, pairs)  7.82 us
    ppermute x2, starting transfers between devices, shifted(): return lax.ppermute(value, axis, pairs)  5.09 us
  transfers between devices with their start and end apart: 3, of which 3 were waited for; matrix products, arithmetic and copies ran while one was open for 0% of the time, Pallas kernels for 0%

profile of v1, /device:TPU:0, one launch (start us, length us, event | category | flops | bytes accessed | tf_op | source)
XLA Modules:
  0.0 75.0 jit_solution(2446186189634155103)
XLA Ops:
  6.5 0.0 copy-start
  6.5 0.0 copy-start.2
  6.5 0.0 copy-start.1
  6.5 0.0 all-gather.3.cloned.1.call-start
  6.5 3.0 %collective-permute-start = (s32[1,1,24]{2,1,0:T(1,128)}, s32[1,1,24]{2,1,0:T(1,128)S(1)}, u32[]{:S(2)}, u32[]{:S(2)}) collective-permute-start(s32[1,1,24]{2,1,0:T(1,128)} %param.6), channel_id=1, source_target_pairs={{0,8},{8,16},{16,24},{24,0},{1,9},{9,17},{17,25},{25,1},{2,10},{10... | collective-permute-start | bytes 296 | tf_op jit(solution)/shard_map/ppermute | solution.py:10
  9.6 2.6 %collective-permute-done = s32[1,1,24]{2,1,0:T(1,128)S(1)} collective-permute-done((s32[1,1,24]{2,1,0:T(1,128)}, s32[1,1,24]{2,1,0:T(1,128)S(1)}, u32[]{:S(2)}, u32[]{:S(2)}) %collective-permute-start) | collective-permute-done | bytes 128 | tf_op jit(solution)/shard_map/ppermute | solution.py:10
  12.2 0.0 copy-done
  12.2 0.7 gather_fusion
  13.0 0.1 broadcast_select_fusion
  13.1 2.1 %collective-permute-start.1 = (bf16[24,6144]{1,0:T(8,128)(2,1)S(1)}, bf16[24,6144]{1,0:T(8,128)(2,1)S(1)}, u32[]{:S(2)}, u32[]{:S(2)}) collective-permute-start(bf16[24,6144]{1,0:T(8,128)(2,1)S(1)} %broadcast_select_fusion), channel_id=1, source_target_pairs={{0,24},{8,0},{16,8},{24,16},{1,25},{9,1},{17,9},{25,17},{2,26},{10... | collective-permute-start | bytes 884744 | tf_op jit(solution)/shard_map/ppermute | solution.py:10
  15.8 0.0 copy-done.2
  15.8 5.2 %collective-permute-done.1 = bf16[24,6144]{1,0:T(8,128)(2,1)S(1)} collective-permute-done((bf16[24,6144]{1,0:T(8,128)(2,1)S(1)}, bf16[24,6144]{1,0:T(8,128)(2,1)S(1)}, u32[]{:S(2)}, u32[]{:S(2)}) %collective-permute-start.1) | collective-permute-done | bytes 294944 | tf_op jit(solution)/shard_map/ppermute | solution.py:10
  21.0 0.8 %multiply_convert_fusion = bf16[24,6144]{1,0:T(8,128)(2,1)} fusion(bf16[24,6144]{1,0:T(8,128)(2,1)S(1)} %collective-permute-done.1, f32[24]{0:T(128)S(1)} %compare_select_fusion.2), kind=kLoop, calls=%fused_computation.2 | loop fusion | flops 442368 | bytes 589920 | tf_op jit(solution)/shard_map/convert_element_type | solution.py:25
  21.8 0.0 all-gather.3.cloned.1.call-update
  21.9 0.0 copy-done.1
  22.0 23.9 %all_to_all.5 = bf16[8,1,1,24,1024]{4,3,2,1,0:T(8,128)(2,1)S(1)} all-to-all(bf16[8,1,1,24,1024]{4,3,2,1,0:T(8,128)(2,1)S(1)} %bitcast_dynamic-update-slice_fusion), channel_id=1, replica_groups=mesh['pipe'=4,'dp'=8] {'dp'}, dimensions={0} | all-to-all | bytes 786432 | tf_op jit(solution)/shard_map/all_to_all | solution.py:27
  45.8 14.0 %all-gather.3.cloned.1.call-done = bf16[192,6144]{1,0:T(8,128)(2,1)} async-done(((bf16[24,6144]{1,0:T(8,128)(2,1)}), bf16[192,6144]{1,0:T(8,128)(2,1)}) %all-gather.3.cloned.1.call-update) | async-done | bytes 2359312 | tf_op jit(solution)/shard_map/all_gather | solution.py:30
  59.8 8.3 %convert_bitcast_fusion = bf16[1,1024,6144]{2,1,0:T(8,128)(2,1)} fusion(bf16[192,1024]{1,0:T(8,128)(2,1)S(1)} %bitcast.33, bf16[192,6144]{1,0:T(8,128)(2,1)} %all-gather.3.cloned.1.call-done), kind=kOutput, calls=%fused_computation.1 | convolution fusion | flops 2422210560 | bytes 15335424 | tf_op jit(solution)/shard_map/dot_general | solution.py:34
  (12 shorter events, 0.1 us)
Async XLA Ops:
  6.5 5.7 %copy-start = (bf16[1,128,6144]{2,1,0:T(8,128)(2,1)S(1)}, bf16[1,128,6144]{2,1,0:T(8,128)(2,1)}, u32[]{:S(2)}) copy-start(bf16[1,128,6144]{2,1,0:T(8,128)(2,1)} %param.5) | copy-start | bytes 4718596
  6.5 9.3 %copy-start.2 = (f32[1,1,24]{2,1,0:T(1,128)S(1)}, f32[1,1,24]{2,1,0:T(1,128)}, u32[]{:S(2)}) copy-start(f32[1,1,24]{2,1,0:T(1,128)} %param.8) | copy-start | bytes 292
  6.5 15.3 %copy-start.1 = (bf16[1,1,24,8192]{3,2,1,0:T(8,128)(2,1)S(1)}, bf16[1,1,24,8192]{3,2,1,0:T(8,128)(2,1)}, u32[]{:S(2)}) copy-start(bf16[1,1,24,8192]{3,2,1,0:T(8,128)(2,1)} %param.9) | copy-start | bytes 1179652
  6.5 53.3 %all-gather.3.cloned.1.call-start = ((), (), s32[]{:S(2)}) async-start(), calls=%async_computation.1 | async-start | bytes 2654208 | tf_op jit(solution)/shard_map/all_gather | solution.py:30
  6.5 5.7 %collective-permute-start = (s32[1,1,24]{2,1,0:T(1,128)}, s32[1,1,24]{2,1,0:T(1,128)S(1)}, u32[]{:S(2)}, u32[]{:S(2)}) collective-permute-start(s32[1,1,24]{2,1,0:T(1,128)} %param.6), channel_id=1, source_target_pairs={{0,8},{8,16},{16,24},{24,0},{1,9},{9,17},{17,25},{25,1},{2,10},{10... | collective-permute-start | bytes 296 | tf_op jit(solution)/shard_map/ppermute | solution.py:10
  13.1 7.9 %collective-permute-start.1 = (bf16[24,6144]{1,0:T(8,128)(2,1)S(1)}, bf16[24,6144]{1,0:T(8,128)(2,1)S(1)}, u32[]{:S(2)}, u32[]{:S(2)}) collective-permute-start(bf16[24,6144]{1,0:T(8,128)(2,1)S(1)} %broadcast_select_fusion), channel_id=1, source_target_pairs={{0,24},{8,0},{16,8},{24,16},{1,25},{9,1},{17,9},{25,17},{2,26},{10... | collective-permute-start | bytes 884744 | tf_op jit(solution)/shard_map/ppermute | solution.py:10
Sparse Core Ops, SparseCore 0:
  22.0 37.8 all-gather.2
